TPU v7x, 256 devices: a whole 4x4x8 slice. The times are simulated.
256 devices in a mesh: gz: 64 (over x, y, z_hi, core), gy: 4 (over z_lo).
Axes of the slice: x: 4, y: 4, z: 8 (z_hi: 2, z_lo: 4; z = z_hi * 4 + z_lo), core: 2. Of those that a mesh axis runs over, the one named last changes fastest.
Arguments:
- velocity: float32 [2, 2, 1536, 7680], P(None, None, 'gz', 'gy'), may hold values from -0.15625 to 0.15625
- vorticity: float32 [2, 2, 1536, 7680], P(None, None, 'gz', 'gy'), may hold values from -0.15625 to 0.15625
Outputs:
- criterion: float32 [2, 4, 1920, 1536], P(None, None, 'gz', 'gy')
All inputs are finite; a program needn't handle non-finite values.
Results may differ from a plain program's by a relative error of at most 0.0003.
Values sent between devices are 32-bit elements; how exact they have to be, the bound alone decides.
No kernel may reach another device: no remote copies, remote signals or barrier semaphores. Data moves between devices by JAX's collectives and lax.ppermute only.
A program may use at most 128 MiB of HBM per device.

v0:
```python
import math

import jax
import jax.numpy as jnp
from jax import lax
from jax.experimental import pallas as pl
from jax.experimental.pallas import tpu as pltpu
from jax.sharding import Mesh
from jax.sharding import PartitionSpec as P


NY = 1536
NZ = 7680
KX = 2
HALF = NY // 2
SLOT = 32
LANES = 128
BLOCKS = (256, 512)
LIMIT = 24 * 1024 * 1024
SPANS = ("x", "y", "half", "core")
ROUTE = ("half", "y", "x", "core")
SIZES = {"x": 4, "y": 4, "half": 2, "core": 2}


def routes():
    places = []
    for a in range(math.prod(SIZES.values())):
        rest, at = a, {}
        for name in reversed(SPANS):
            rest, at[name] = divmod(rest, SIZES[name])
        place = 0
        for name in ROUTE:
            place = place * SIZES[name] + at[name]
        places.append(place)
    return places


def spanwise(index):
    signed = jnp.where(index < NZ // 2, index, index - NZ)
    return signed.astype(jnp.float32) * (2.0 / NZ)


def pack_kernel(places, cols, v_hbm, o_hbm, out_hbm, v_buf, o_buf, out_ref, sems):
    _, modes, rows, span = v_buf.shape
    chunks = span // LANES
    copies = []
    for t in range(rows // 8):
        at = pl.ds(8 * t, 8)
        pair = [
            pltpu.make_async_copy(src.at[:, :, at, :], dst.at[:, :, at, :], sems.at[t, f])
            for f, (src, dst) in enumerate(((v_hbm, v_buf), (o_hbm, o_buf)))
        ]
        for copy in pair:
            copy.start()
        copies.append(pair)
    lane = lax.broadcasted_iota(jnp.int32, (8, LANES), 1)
    leaving = []
    for t in range(rows // 8):
        at = pl.ds(8 * t, 8)
        for copy in copies[t]:
            copy.wait()
        turned = {}

        def tile(m, g, k):
            if (m, g, k) not in turned:
                ref = (v_buf, o_buf)[g // 2]
                value = ref[g % 2, m, at, pl.ds(LANES * (k % chunks), LANES)]
                turned[m, g, k] = pltpu.roll(value, SLOT * g, 1) if g else value
            return turned[m, g, k]

        for a, place in enumerate(places):
            k, off = divmod(cols * a, LANES)
            own = (lane - off) & (LANES - 1)
            for m in range(modes):
                merged = [tile(m, 0, k + s) for s in range(2 if off + cols > LANES else 1)]
                for g in range(1, 4):
                    merged = [jnp.where(own >= SLOT * g, tile(m, g, k + s), v) for s, v in enumerate(merged)]
                value = merged[0]
                if len(merged) > 1:
                    value = jnp.where((own & (SLOT - 1)) < LANES - off, value, merged[1])
                out_ref[place, pl.ds(8 * t * modes + m, 8, stride=modes), :] = value
        done = pl.ds(8 * t * modes, 8 * modes)
        leaving.append(pltpu.make_async_copy(out_ref.at[:, done, :], out_hbm.at[:, done, :], sems.at[t, 2]))
        leaving[-1].start()
    for copy in leaving:
        copy.wait()


def pack(velocity, vorticity, places):
    _, modes, rows, span = velocity.shape
    peers = len(places)
    return pl.pallas_call(
        lambda *refs: pack_kernel(places, span // peers, *refs),
        in_specs=[pl.BlockSpec(memory_space=pltpu.HBM)] * 2,
        out_specs=pl.BlockSpec(memory_space=pltpu.HBM),
        out_shape=jax.ShapeDtypeStruct((peers, rows * modes, LANES), jnp.float32),
        scratch_shapes=[pltpu.VMEM(velocity.shape, jnp.float32)] * 2
        + [pltpu.VMEM((peers, rows * modes, LANES), jnp.float32), pltpu.SemaphoreType.DMA((rows // 8, 3))],
        compiler_params=pltpu.CompilerParams(vmem_limit_bytes=LIMIT),
        name="pack",
    )(*(pltpu.with_memory_space_constraint(x, pltpu.HBM) for x in (velocity, vorticity)))


def table_kernel(base_ref, hi_ref, lo_ref):
    rows = 32

    def block(i, carry):
        at = pl.ds(pl.multiple_of(i * rows, rows), rows)
        for parity in range(2):
            c, s, turn_c, turn_s = (base_ref[parity, k, at, :] for k in range(4))
            for q in range(HALF // LANES):
                lanes = pl.ds(LANES * q, LANES)
                hi_ref[parity, at, lanes], lo_ref[parity, at, lanes] = halves_of(c)
                c, s = c * turn_c - s * turn_s, s * turn_c + c * turn_s
        return carry

    lax.fori_loop(0, HALF // rows, block, 0)


def tables():
    point = jnp.arange(HALF, dtype=jnp.int32)[:, None]
    first = 2 * jnp.arange(LANES, dtype=jnp.int32)[None, :]
    turn = jnp.full((1, LANES), 2 * LANES, jnp.int32)

    def angle(degree):
        return (degree * (2 * point + 1) % (4 * NY)).astype(jnp.float32) * (math.pi / (2 * NY))

    degrees = jnp.stack([angle(first), angle(first + 1)])
    turns = jnp.broadcast_to(angle(turn), degrees.shape)
    base = jnp.stack([jnp.cos(degrees), jnp.sin(degrees), jnp.cos(turns), jnp.sin(turns)], axis=1)
    return pl.pallas_call(
        table_kernel,
        out_shape=[jax.ShapeDtypeStruct((2, HALF, HALF), jnp.bfloat16)] * 2,
        compiler_params=pltpu.CompilerParams(vmem_limit_bytes=LIMIT),
        name="tables",
    )(base)


def factors(own, first):
    normal = own < 2 * SLOT
    wave_z = spanwise(first + own % SLOT)
    wave_x = (jnp.arange(KX, dtype=jnp.int32) + 1).astype(jnp.float32) / KX
    wave = wave_x[:, None] * wave_x[:, None] + wave_z[None, :] * wave_z[None, :]
    degree = jnp.arange(NY, dtype=jnp.int32).reshape(HALF, 2).T.astype(jnp.float32)
    scaled = degree * (math.pi / NY)
    stretch = (scaled * jnp.sin(scaled))[:, :, None]
    edge = (-0.5 * scaled * jnp.sin(0.5 * scaled))[:, :, None]
    by_degree = jnp.where(normal, jnp.stack([stretch, edge]), 0.0)
    shift = jnp.where(normal, wave, 1.0)
    size = jnp.where(normal, 0.5 * lax.rsqrt(wave), 0.5)
    slope = jnp.where(normal, 0.0, 0.25 / wave)
    rows = jnp.broadcast_to(jnp.stack([shift * size, size, slope], axis=1)[:, :, None, :], (KX, 3, 8, LANES))
    lane = jnp.arange(LANES, dtype=jnp.int32)
    part = jnp.arange(2 * KX, dtype=jnp.int32)
    pick = (own[None, :, None] % SLOT == lane % SLOT) & (lane // SLOT == part[:, None, None])
    pick = pick.reshape(2 * KX * LANES, LANES)
    flip = lane[:, None] + lane[None, :] == LANES - 1
    return by_degree, rows, pick.astype(jnp.bfloat16), flip.astype(jnp.bfloat16)


def halves_of(value):
    high = value.astype(jnp.bfloat16)
    return high, (value - high.astype(jnp.float32)).astype(jnp.bfloat16)


def product(a, b):
    return jnp.dot(a, b, preferred_element_type=jnp.float32)


def criterion_kernel(
    places, peers, me_ref, x_ref, hi_hbm, lo_hbm, degree_ref, rows_ref, pick_ref, flip_ref, *refs
):
    outs, (hi_ref, lo_ref, xh_ref, xl_ref, low_ref, top_ref, vh_ref, vl_ref, res_ref, out_ref, sems) = (
        refs[:peers],
        refs[peers:],
    )
    copies = [
        [
            pltpu.make_async_copy(src.at[:, at, :], dst.at[:, at, :], sems.at[b, k])
            for k, (src, dst) in enumerate(((hi_hbm, hi_ref), (lo_hbm, lo_ref)))
        ]
        for b, at in enumerate(pl.ds(sum(BLOCKS[:b]), size) for b, size in enumerate(BLOCKS))
    ]
    for copy in sum(copies, []):
        copy.start()
    modes = x_ref.shape[0] // NY
    pair = 2 * NY // len(places)
    half = pair // 2
    totals = [jnp.zeros((half, LANES), jnp.float32) for _ in range(2 * modes)]
    for parity in range(2):
        for m in range(modes):
            lanes = pl.ds(LANES * m, LANES)
            shift, size = rows_ref[m, 0, :1], rows_ref[m, 1, :1]
            for row in range(0, HALF, half):
                at = pl.ds(row, half)
                first = places[2 * row // half] * half * modes + parity * modes + m
                x = x_ref[pl.ds(first, half, stride=2 * modes), :]
                totals[parity * modes + m] = totals[parity * modes + m] + x * degree_ref[1, parity, at, :]
                high, low = halves_of(x * (shift + size * degree_ref[0, parity, at, :]))
                xh_ref[parity, at, lanes] = high
                xl_ref[parity, at, lanes] = low
    outside = jnp.zeros((8, LANES * modes), jnp.float32)
    low_ref[pl.ds(0, 8), :] = outside
    top_ref[pl.ds(0, 8), :] = outside

    def values(start, size):
        at = pl.ds(start, size)
        for part in range(2 * modes):
            ref, m = (low_ref, top_ref)[part // modes], part % modes
            lanes = pl.ds(LANES * m, LANES)
            here = ref[pl.ds(8 + start, size), lanes]
            slope = ref[pl.ds(9 + start, size), lanes] - ref[pl.ds(7 + start, size), lanes]
            high, low = halves_of(here * here + slope * slope * rows_ref[m, 2, :1])
            vh_ref[at, pl.ds(LANES * part, LANES)] = high
            vl_ref[at, pl.ds(LANES * part, LANES)] = low
        res_ref[at, :] = product(vh_ref[at, :], pick_ref[...]) + product(vl_ref[at, :], pick_ref[...])

    done = 0
    for block, rows in enumerate(BLOCKS):
        start = sum(BLOCKS[:block])
        at = pl.ds(start, rows)
        for copy in copies[block]:
            copy.wait()
        halves = []
        for parity in range(2):
            xh = xh_ref[parity]
            halves.append(
                product(hi_ref[parity, at, :], xh) + product(hi_ref[parity, at, :], xl_ref[parity]) + product(lo_ref[parity, at, :], xh)
            )
        low_ref[pl.ds(8 + start, rows), :] = halves[0] + halves[1]
        top_ref[pl.ds(8 + start, rows), :] = halves[0] - halves[1]
        if start == 0:
            for m in range(modes):
                lanes = pl.ds(LANES * m, LANES)
                even, odd = (
                    rows_ref[m, 1, :1] * jnp.sum(totals[parity * modes + m], axis=0, keepdims=True) for parity in range(2)
                )
                low_ref[pl.ds(8, 1), lanes] = low_ref[pl.ds(8, 1), lanes] + (even + odd)
                top_ref[pl.ds(8, 1), lanes] = top_ref[pl.ds(8, 1), lanes] + (even - odd)
        if start + rows == HALF:
            low_ref[pl.ds(8 + HALF, 1), :] = top_ref[pl.ds(7 + HALF, 1), :]
            top_ref[pl.ds(8 + HALF, 1), :] = low_ref[pl.ds(7 + HALF, 1), :]
        ready = start + rows - (8 if start + rows < HALF else 0)
        while done < ready:
            size = min(LANES, ready - done)
            values(done, size)
            done += size
    above = []
    for b in range(HALF // LANES):
        turned = res_ref[pl.ds(LANES * b, LANES), :].T
        peer, at = divmod(LANES * b, out_ref.shape[-1])
        out_ref[peer, :, pl.ds(at, LANES)] = turned[: SLOT * modes]
        above.append(turned[SLOT * modes :])
    high, low = halves_of(jnp.concatenate(above, axis=0))
    above = product(high, flip_ref[...]) + product(low, flip_ref[...])
    for b in range(HALF // LANES):
        peer, at = divmod(NY - LANES * (b + 1), out_ref.shape[-1])
        out_ref[peer, :, pl.ds(at, LANES)] = above[SLOT * modes * b : SLOT * modes * (b + 1)]
    for d, out in enumerate(outs):
        out[...] = out_ref[me_ref[0] ^ d]


def criterion(me, field, high, low, numbers, places, peers):
    modes = field.shape[1] * len(places) // NY
    width = LANES * modes
    fast, slow = pl.BlockSpec(memory_space=pltpu.VMEM), pl.BlockSpec(memory_space=pltpu.HBM)
    call = pl.pallas_call(
        lambda *refs: criterion_kernel(places, peers, *refs),
        in_specs=[pl.BlockSpec(memory_space=pltpu.SMEM), fast, slow, slow, fast, fast, fast, fast],
        out_specs=[fast] * peers,
        out_shape=[pltpu.VMEM((SLOT * modes, NY // peers), jnp.float32)] * peers,
        scratch_shapes=[pltpu.VMEM(high.shape, jnp.bfloat16)] * 2
        + [pltpu.VMEM((2, HALF, width), jnp.bfloat16)] * 2
        + [pltpu.VMEM((HALF + 16, width), jnp.float32)] * 2
        + [pltpu.VMEM((HALF, 2 * width), jnp.bfloat16)] * 2
        + [pltpu.VMEM((HALF, LANES), jnp.float32), pltpu.VMEM((peers, SLOT * modes, NY // peers), jnp.float32)]
        + [pltpu.SemaphoreType.DMA((len(BLOCKS), 2))],
        compiler_params=pltpu.CompilerParams(vmem_limit_bytes=LIMIT),
        name="criterion",
    )
    high, low = (pltpu.with_memory_space_constraint(x, pltpu.HBM) for x in (high, low))
    return call(me[None], field.reshape(NY * modes, LANES), high, low, *numbers)


def assemble_kernel(me_ref, *refs):
    parts, out_ref = refs[:-1], refs[-1]
    modes, columns, senders, _ = out_ref.shape
    for d, part in enumerate(parts):
        for q in range(senders):

            @pl.when((me_ref[0] ^ d) == q)
            def _():
                for m in range(modes):
                    out_ref[m, :, q, :] = part[pl.ds(SLOT * m, columns), :]


def assemble(me, parts, columns):
    modes = parts[0].shape[0] // SLOT
    fast = pl.BlockSpec(memory_space=pltpu.VMEM)
    return pl.pallas_call(
        assemble_kernel,
        in_specs=[pl.BlockSpec(memory_space=pltpu.SMEM)] + [fast] * len(parts),
        out_shape=jax.ShapeDtypeStruct((modes, columns, len(parts), parts[0].shape[1]), jnp.float32),
        compiler_params=pltpu.CompilerParams(vmem_limit_bytes=LIMIT),
        name="assemble",
    )(me[None], *parts)


def local(velocity, vorticity):
    walls = lax.axis_size("gy")
    places = routes()
    columns = NZ // (len(places) * walls)
    sent = pack(velocity, vorticity, places)
    field = lax.all_to_all(sent, ROUTE, split_axis=0, concat_axis=0, tiled=True)
    high, low = tables()
    start = lax.axis_index(SPANS) * columns
    own = (jnp.arange(LANES, dtype=jnp.int32) - start) % LANES
    numbers = factors(own, lax.axis_index("gy") * (NZ // walls) + start)
    me = lax.axis_index("gy")
    parts = list(criterion(me, field, high, low, numbers, places, walls))
    for d in range(1, walls):
        parts[d] = lax.ppermute(parts[d], "gy", [(i, i ^ d) for i in range(walls)])
    return jnp.moveaxis(assemble(me, parts, columns), 2, 1)


def solution(mesh):
    fine = Mesh(mesh.devices.reshape(*SIZES.values(), -1), (*SIZES, "gy"))
    placed = P(None, None, SPANS, "gy")
    return jax.shard_map(
        local, mesh=fine, in_specs=(placed, placed), out_specs=placed, check_vma=False
    )
```

profile of v0, /device:TPU:6, one launch (start us, length us, event | category | flops | bytes accessed | tf_op | source)
XLA Modules:
  0.0 77.0 jit_solution(14910410193837118958)
XLA Ops:
  0.0 2.6 %pack.1 = f32[64,48,128]{2,1,0:T(8,128)} custom-call(f32[2,2,24,1920]{3,2,1,0:T(8,128)} %refs_0_.1, f32[2,2,24,1920]{3,2,1,0:T(8,128)} %refs_1_.1), custom_call_target="tpu_custom_call" | custom-call | tf_op jit(solution)/shard_map/pack/pallas_call | solution.py:92
  2.6 14.6 %all-to-all-start = ((f32[64,48,128]{2,1,0:T(8,128)}), f32[64,48,128]{2,1,0:T(8,128)S(1)}, u32[]{:S(2)}, u32[]{:S(2)}) async-start(f32[64,48,128]{2,1,0:T(8,128)} %pack.1), calls=%async_computation | async-start | bytes 3145728 | tf_op jit(solution)/shard_map/all_to_all | solution.py:314
  17.3 0.5 fusion.4
  17.8 2.8 %fusion.1 = (f32[2,1,768,128]{3,2,1,0:T(8,128)S(1)}, f32[2,1,768,128]{3,2,1,0:T(8,128)S(1)}) fusion(f32[1,1,768,128]{3,2,1,0:T(8,128)S(1)} %get-tuple-element.22, f32[1,1,768,128]{3,2,1,0:T(8,128)S(1)} %get-tuple-element.21), kind=kLoop, calls=%fused_computation.4 | loop fusion | flops 196608 | bytes 2359296 | tf_op jit(solution)/shard_map/cos | solution.py:130
  20.6 1.5 %fusion.9 = (f32[768,128]{1,0:T(8,128)S(1)}, f32[768,128]{1,0:T(8,128)S(1)}) fusion(s32[768]{0:T(1024)S(1)} %get-tuple-element.26, s32[768]{0:T(1024)S(1)} %get-tuple-element.27, pred[768]{0:T(1024)(128)(4,1)S(1)} %compare_and_fusion), kind=kLoop, calls=%fused_computation.15 | loop fusion | flops 294912 | bytes 793344 | tf_op jit(solution)/shard_map/cos | solution.py:130
  22.2 0.1 stack.33
  22.2 0.1 stack.32
  22.3 0.2 pad_maximum_fusion.base_ref
  22.5 1.6 %tables.1 = (bf16[2,768,768]{2,1,0:T(8,128)(2,1)S(1)}, bf16[2,768,768]{2,1,0:T(8,128)(2,1)S(1)}) custom-call(f32[2,4,768,128]{3,2,1,0:T(8,128)S(1)} %pad_maximum_fusion.base_ref), custom_call_target="tpu_custom_call" | custom-call | tf_op jit(solution)/shard_map/tables/pallas_call | solution.py:131
  24.1 0.0 copy-start
  24.1 1.4 %copy-done = bf16[2,768,768]{2,1,0:T(8,128)(2,1)} copy-done((bf16[2,768,768]{2,1,0:T(8,128)(2,1)}, bf16[2,768,768]{2,1,0:T(8,128)(2,1)S(1)}, u32[]{:S(2)}) %copy-start) | copy-done | bytes 2359320
  25.5 0.0 copy-start.1
  25.5 1.4 %copy-done.1 = bf16[2,768,768]{2,1,0:T(8,128)(2,1)} copy-done((bf16[2,768,768]{2,1,0:T(8,128)(2,1)}, bf16[2,768,768]{2,1,0:T(8,128)(2,1)S(1)}, u32[]{:S(2)}) %copy-start.1) | copy-done | bytes 2359320
  27.0 0.1 fusion.18
  27.1 0.2 sine_multiply_fusion
  27.4 0.1 broadcast_compare_fusion
  27.5 0.5 broadcast_select_fusion.refs_4_
  28.0 28.5 %all-to-all-done = f32[64,48,128]{2,1,0:T(8,128)S(1)} async-done(((f32[64,48,128]{2,1,0:T(8,128)}), f32[64,48,128]{2,1,0:T(8,128)S(1)}, u32[]{:S(2)}, u32[]{:S(2)}) %all-to-all-start) | async-done | bytes 1572896 | tf_op jit(solution)/shard_map/all_to_all | solution.py:314
  56.5 5.1 %criterion.1 = (f32[64,384]{1,0:T(8,128)S(1)}, f32[64,384]{1,0:T(8,128)S(1)}, f32[64,384]{1,0:T(8,128)S(1)}, f32[64,384]{1,0:T(8,128)S(1)}) custom-call(s32[1]{0:T(128)} %bitcast.refs_0_.me_ref, f32[3072,128]{1,0:T(8,128)S(1)} %bitcast.10, bf16[2,768,768]{2,1,0:T(8,128)(2,1)} %copy-done, bf16[2,768,768]{2,1,0:T(8,128)(2,1)} %copy-done.1, ...), custom_call_target="tpu_custom_call" | custom-call | tf_op jit(solution)/shard_map/criterion/pallas_call | solution.py:282
  61.6 4.0 %collective-permute-start = (f32[64,384]{1,0:T(8,128)S(1)}, f32[64,384]{1,0:T(8,128)S(1)}, u32[]{:S(2)}, u32[]{:S(2)}) collective-permute-start(f32[64,384]{1,0:T(8,128)S(1)} %get-tuple-element.14), channel_id=1, source_target_pairs={{0,1},{1,0},{2,3},{3,2},{4,5},{5,4},{6,7},{7,6},{8,9},{9,8},{10,11... | collective-permute-start | bytes 294920 | tf_op jit(solution)/shard_map/ppermute | solution.py:322
  65.5 0.6 collective-permute-start.1
  66.1 1.9 %collective-permute-start.2 = (f32[64,384]{1,0:T(8,128)S(1)}, f32[64,384]{1,0:T(8,128)S(1)}, u32[]{:S(2)}, u32[]{:S(2)}) collective-permute-start(f32[64,384]{1,0:T(8,128)S(1)} %get-tuple-element.16), channel_id=1, source_target_pairs={{0,3},{1,2},{2,1},{3,0},{4,7},{5,6},{6,5},{7,4},{8,11},{9,10},{10,... | collective-permute-start | bytes 294920 | tf_op jit(solution)/shard_map/ppermute | solution.py:322
  68.0 0.7 collective-permute-done.refs_1_
  68.7 7.3 %collective-permute-done.1.refs_2_ = f32[64,384]{1,0:T(8,128)S(1)} collective-permute-done((f32[64,384]{1,0:T(8,128)S(1)}, f32[64,384]{1,0:T(8,128)S(1)}, u32[]{:S(2)}, u32[]{:S(2)}) %collective-permute-start.1) | collective-permute-done | bytes 98336 | tf_op jit(solution)/shard_map/ppermute | solution.py:322
  76.0 0.0 collective-permute-done.2.refs_3_
  76.0 1.0 %assemble.1 = f32[2,30,4,384]{3,2,1,0:T(4,128)} custom-call(s32[1]{0:T(128)} %bitcast.refs_0_.me_ref, f32[64,384]{1,0:T(8,128)S(1)} %get-tuple-element.13.refs_0_, f32[64,384]{1,0:T(8,128)S(1)} %collective-permute-done.refs_1_, f32[64,384]{1,0:T(8,128)S(1)} %collective-permute-done.1.refs_2_, f32[64,384]{1,0:T(8,128)S(1)} %collective-permute-done.2.refs_3_), custom_call_target="tpu_custom_call" | custom-call | tf_op jit(solution)/shard_map/assemble/pallas_call | solution.py:300
  (15 shorter events, 0.2 us)
Async XLA Ops:
  2.6 53.8 %all-to-all-start = ((f32[64,48,128]{2,1,0:T(8,128)}), f32[64,48,128]{2,1,0:T(8,128)S(1)}, u32[]{:S(2)}, u32[]{:S(2)}) async-start(f32[64,48,128]{2,1,0:T(8,128)} %pack.1), calls=%async_computation | async-start | bytes 3145728 | tf_op jit(solution)/shard_map/all_to_all | solution.py:314
  24.1 1.4 %copy-start = (bf16[2,768,768]{2,1,0:T(8,128)(2,1)}, bf16[2,768,768]{2,1,0:T(8,128)(2,1)S(1)}, u32[]{:S(2)}) copy-start(bf16[2,768,768]{2,1,0:T(8,128)(2,1)S(1)} %get-tuple-element.11.refs_2_) | copy-start | bytes 7077892
  25.5 1.4 %copy-start.1 = (bf16[2,768,768]{2,1,0:T(8,128)(2,1)}, bf16[2,768,768]{2,1,0:T(8,128)(2,1)S(1)}, u32[]{:S(2)}) copy-start(bf16[2,768,768]{2,1,0:T(8,128)(2,1)S(1)} %get-tuple-element.12.refs_3_) | copy-start | bytes 7077892
  61.6 7.2 %collective-permute-start = (f32[64,384]{1,0:T(8,128)S(1)}, f32[64,384]{1,0:T(8,128)S(1)}, u32[]{:S(2)}, u32[]{:S(2)}) collective-permute-start(f32[64,384]{1,0:T(8,128)S(1)} %get-tuple-element.14), channel_id=1, source_target_pairs={{0,1},{1,0},{2,3},{3,2},{4,5},{5,4},{6,7},{7,6},{8,9},{9,8},{10,11... | collective-permute-start | bytes 294920 | tf_op jit(solution)/shard_map/ppermute | solution.py:322
  65.5 10.5 %collective-permute-start.1 = (f32[64,384]{1,0:T(8,128)S(1)}, f32[64,384]{1,0:T(8,128)S(1)}, u32[]{:S(2)}, u32[]{:S(2)}) collective-permute-start(f32[64,384]{1,0:T(8,128)S(1)} %get-tuple-element.15), channel_id=1, source_target_pairs={{0,2},{1,3},{2,0},{3,1},{4,6},{5,7},{6,4},{7,5},{8,10},{9,11},{10,... | collective-permute-start | bytes 294920 | tf_op jit(solution)/shard_map/ppermute | solution.py:322
  66.1 10.0 %collective-permute-start.2 = (f32[64,384]{1,0:T(8,128)S(1)}, f32[64,384]{1,0:T(8,128)S(1)}, u32[]{:S(2)}, u32[]{:S(2)}) collective-permute-start(f32[64,384]{1,0:T(8,128)S(1)} %get-tuple-element.16), channel_id=1, source_target_pairs={{0,3},{1,2},{2,1},{3,0},{4,7},{5,6},{6,5},{7,4},{8,11},{9,10},{10,... | collective-permute-start | bytes 294920 | tf_op jit(solution)/shard_map/ppermute | solution.py:322
where the time goes:
time: 77.5 us; the launch traced here: 77 us
  waiting for transfers between devices  36.6 us (47%)
  starting transfers between devices  21 us (27%)
  Pallas kernels  10.2 us (13%)
  other arithmetic  6.03 us (8%)
  local copies, waits for them, and re-layouts  2.95 us (4%)
    all_to_all x1, waiting for transfers between devices, local(): field = lax.all_to_all(sent, ROUTE, split_axis=0, concat_axis=0, tiled=True)  28.5 us
    all_to_all x1, starting transfers between devices, local(): field = lax.all_to_all(sent, ROUTE, split_axis=0, concat_axis=0, tiled=True)  14.6 us
    ppermute x3, waiting for transfers between devices, local(): parts[d] = lax.ppermute(parts[d], 'gy', [(i, i ^ d) for i in range(walls)])  8.05 us
    ppermute x3, starting transfers between devices, local(): parts[d] = lax.ppermute(parts[d], 'gy', [(i, i ^ d) for i in range(walls)])  6.44 us
    pallas_call x1, Pallas kernels, criterion(): return call(me[None], field.reshape(NY * modes, LANES), high, low, *numbers)  5.08 us
    unnamed x4, local copies, waits for them, and re-layouts  2.85 us
    cos x1, other arithmetic, tables(): jnp.cos(degrees)  2.78 us
    pallas_call x1, Pallas kernels, pack(): pl.pallas_call(lambda *refs: pack_kernel(places, span // peers, *refs), i...  2.63 us
  transfers between devices with their start and end apart: 4, of which 3 were waited for; matrix products, arithmetic and copies ran while one was open for 8% of the time, Pallas kernels for 2%

commit v1 on v0

--- a/solution.py
+++ b/solution.py
@@ -136,7 +136,7 @@
     )(base)
 
 
-def factors(own, first):
+def factors(own, first, columns):
     normal = own < 2 * SLOT
     wave_z = spanwise(first + own % SLOT)
     wave_x = (jnp.arange(KX, dtype=jnp.int32) + 1).astype(jnp.float32) / KX
@@ -152,7 +152,8 @@
     rows = jnp.broadcast_to(jnp.stack([shift * size, size, slope], axis=1)[:, :, None, :], (KX, 3, 8, LANES))
     lane = jnp.arange(LANES, dtype=jnp.int32)
     part = jnp.arange(2 * KX, dtype=jnp.int32)
-    pick = (own[None, :, None] % SLOT == lane % SLOT) & (lane // SLOT == part[:, None, None])
+    target = part[:, None] // KX * (SLOT * KX) + part[:, None] % KX * columns + own % SLOT
+    pick = (target[:, :, None] == lane) & (own % SLOT < columns)[None, :, None]
     pick = pick.reshape(2 * KX * LANES, LANES)
     flip = lane[:, None] + lane[None, :] == LANES - 1
     return by_degree, rows, pick.astype(jnp.bfloat16), flip.astype(jnp.bfloat16)
@@ -245,35 +246,38 @@
             size = min(LANES, ready - done)
             values(done, size)
             done += size
+    sent = modes * (NZ // (len(places) * peers))
     above = []
     for b in range(HALF // LANES):
         turned = res_ref[pl.ds(LANES * b, LANES), :].T
-        peer, at = divmod(LANES * b, out_ref.shape[-1])
-        out_ref[peer, :, pl.ds(at, LANES)] = turned[: SLOT * modes]
+        peer, at = divmod(LANES * b, NY // peers)
+        out_ref[peer, pl.ds(at // LANES * sent, sent), :] = turned[:sent]
         above.append(turned[SLOT * modes :])
     high, low = halves_of(jnp.concatenate(above, axis=0))
     above = product(high, flip_ref[...]) + product(low, flip_ref[...])
     for b in range(HALF // LANES):
-        peer, at = divmod(NY - LANES * (b + 1), out_ref.shape[-1])
-        out_ref[peer, :, pl.ds(at, LANES)] = above[SLOT * modes * b : SLOT * modes * (b + 1)]
+        peer, at = divmod(NY - LANES * (b + 1), NY // peers)
+        out_ref[peer, pl.ds(at // LANES * sent, sent), :] = above[SLOT * modes * b : SLOT * modes * b + sent]
     for d, out in enumerate(outs):
         out[...] = out_ref[me_ref[0] ^ d]
 
 
 def criterion(me, field, high, low, numbers, places, peers):
+    points = NY // peers // LANES
     modes = field.shape[1] * len(places) // NY
     width = LANES * modes
+    sent = -(-points * modes * (NZ // (len(places) * peers)) // 8) * 8
     fast, slow = pl.BlockSpec(memory_space=pltpu.VMEM), pl.BlockSpec(memory_space=pltpu.HBM)
     call = pl.pallas_call(
         lambda *refs: criterion_kernel(places, peers, *refs),
         in_specs=[pl.BlockSpec(memory_space=pltpu.SMEM), fast, slow, slow, fast, fast, fast, fast],
         out_specs=[fast] * peers,
-        out_shape=[pltpu.VMEM((SLOT * modes, NY // peers), jnp.float32)] * peers,
+        out_shape=[pltpu.VMEM((sent, LANES), jnp.float32)] * peers,
         scratch_shapes=[pltpu.VMEM(high.shape, jnp.bfloat16)] * 2
         + [pltpu.VMEM((2, HALF, width), jnp.bfloat16)] * 2
         + [pltpu.VMEM((HALF + 16, width), jnp.float32)] * 2
         + [pltpu.VMEM((HALF, 2 * width), jnp.bfloat16)] * 2
-        + [pltpu.VMEM((HALF, LANES), jnp.float32), pltpu.VMEM((peers, SLOT * modes, NY // peers), jnp.float32)]
+        + [pltpu.VMEM((HALF, LANES), jnp.float32), pltpu.VMEM((peers, sent, LANES), jnp.float32)]
         + [pltpu.SemaphoreType.DMA((len(BLOCKS), 2))],
         compiler_params=pltpu.CompilerParams(vmem_limit_bytes=LIMIT),
         name="criterion",
@@ -284,23 +288,24 @@
 
 def assemble_kernel(me_ref, *refs):
     parts, out_ref = refs[:-1], refs[-1]
-    modes, columns, senders, _ = out_ref.shape
+    modes, columns, senders, points = out_ref.shape
     for d, part in enumerate(parts):
         for q in range(senders):
 
             @pl.when((me_ref[0] ^ d) == q)
             def _():
                 for m in range(modes):
-                    out_ref[m, :, q, :] = part[pl.ds(SLOT * m, columns), :]
+                    for t in range(points // LANES):
+                        out_ref[m, :, q, pl.ds(LANES * t, LANES)] = part[pl.ds((modes * t + m) * columns, columns), :]
 
 
 def assemble(me, parts, columns):
-    modes = parts[0].shape[0] // SLOT
+    points = NY // len(parts)
     fast = pl.BlockSpec(memory_space=pltpu.VMEM)
     return pl.pallas_call(
         assemble_kernel,
         in_specs=[pl.BlockSpec(memory_space=pltpu.SMEM)] + [fast] * len(parts),
-        out_shape=jax.ShapeDtypeStruct((modes, columns, len(parts), parts[0].shape[1]), jnp.float32),
+        out_shape=jax.ShapeDtypeStruct((KX, columns, len(parts), points), jnp.float32),
         compiler_params=pltpu.CompilerParams(vmem_limit_bytes=LIMIT),
         name="assemble",
     )(me[None], *parts)
@@ -315,7 +320,7 @@
     high, low = tables()
     start = lax.axis_index(SPANS) * columns
     own = (jnp.arange(LANES, dtype=jnp.int32) - start) % LANES
-    numbers = factors(own, lax.axis_index("gy") * (NZ // walls) + start)
+    numbers = factors(own, lax.axis_index("gy") * (NZ // walls) + start, columns)
     me = lax.axis_index("gy")
     parts = list(criterion(me, field, high, low, numbers, places, walls))
     for d in range(1, walls):

time: 77.5 us -> 77.3 us (level)
  no operation moved by 1% of the time
where the time goes in v1:
time: 77.3 us; the launch traced here: 76.9 us
  waiting for transfers between devices  36.1 us (47%)
  starting transfers between devices  21 us (27%)
  Pallas kernels  10.4 us (13%)
  other arithmetic  6.21 us (8%)
  local copies, waits for them, and re-layouts  2.95 us (4%)
    all_to_all x1, waiting for transfers between devices, local(): field = lax.all_to_all(sent, ROUTE, split_axis=0, concat_axis=0, tiled=True)  28.3 us
    all_to_all x1, starting transfers between devices, local(): field = lax.all_to_all(sent, ROUTE, split_axis=0, concat_axis=0, tiled=True)  14.6 us
    ppermute x3, waiting for transfers between devices, local(): parts[d] = lax.ppermute(parts[d], 'gy', [(i, i ^ d) for i in range(walls)])  7.73 us
    ppermute x3, starting transfers between devices, local(): parts[d] = lax.ppermute(parts[d], 'gy', [(i, i ^ d) for i in range(walls)])  6.44 us
    pallas_call x1, Pallas kernels, criterion(): return call(me[None], field.reshape(NY * modes, LANES), high, low, *numbers)  5.09 us
    unnamed x4, local copies, waits for them, and re-layouts  2.84 us
    cos x1, other arithmetic, tables(): jnp.cos(degrees)  2.78 us
    pallas_call x1, Pallas kernels, pack(): pl.pallas_call(lambda *refs: pack_kernel(places, span // peers, *refs), i...  2.7 us
  transfers between devices with their start and end apart: 4, of which 3 were waited for; matrix products, arithmetic and copies ran while one was open for 8% of the time, Pallas kernels for 2%

profile of v1, /device:TPU:6, one launch (start us, length us, event | category | flops | bytes accessed | tf_op | source)
XLA Modules:
  0.0 76.9 jit_solution(5893359127139037502)
XLA Ops:
  0.0 2.7 %pack.1 = f32[64,48,128]{2,1,0:T(8,128)} custom-call(f32[2,2,24,1920]{3,2,1,0:T(8,128)} %refs_0_.1, f32[2,2,24,1920]{3,2,1,0:T(8,128)} %refs_1_.1), custom_call_target="tpu_custom_call" | custom-call | tf_op jit(solution)/shard_map/pack/pallas_call | solution.py:92
  2.7 14.6 %all-to-all-start = ((f32[64,48,128]{2,1,0:T(8,128)}), f32[64,48,128]{2,1,0:T(8,128)S(1)}, u32[]{:S(2)}, u32[]{:S(2)}) async-start(f32[64,48,128]{2,1,0:T(8,128)} %pack.1), calls=%async_computation | async-start | bytes 3145728 | tf_op jit(solution)/shard_map/all_to_all | solution.py:319
  17.4 0.5 fusion.4
  17.9 2.8 %fusion.1 = (f32[2,1,768,128]{3,2,1,0:T(8,128)S(1)}, f32[2,1,768,128]{3,2,1,0:T(8,128)S(1)}) fusion(f32[1,1,768,128]{3,2,1,0:T(8,128)S(1)} %get-tuple-element.22, f32[1,1,768,128]{3,2,1,0:T(8,128)S(1)} %get-tuple-element.21), kind=kLoop, calls=%fused_computation.4 | loop fusion | flops 196608 | bytes 2359296 | tf_op jit(solution)/shard_map/cos | solution.py:130
  20.7 1.5 %fusion.9 = (f32[768,128]{1,0:T(8,128)S(1)}, f32[768,128]{1,0:T(8,128)S(1)}) fusion(s32[768]{0:T(1024)S(1)} %get-tuple-element.26, s32[768]{0:T(1024)S(1)} %get-tuple-element.27, pred[768]{0:T(1024)(128)(4,1)S(1)} %compare_and_fusion), kind=kLoop, calls=%fused_computation.15 | loop fusion | flops 294912 | bytes 793344 | tf_op jit(solution)/shard_map/cos | solution.py:130
  22.2 0.1 stack.33
  22.3 0.1 stack.32
  22.4 0.2 pad_maximum_fusion.base_ref
  22.6 1.6 %tables.1 = (bf16[2,768,768]{2,1,0:T(8,128)(2,1)S(1)}, bf16[2,768,768]{2,1,0:T(8,128)(2,1)S(1)}) custom-call(f32[2,4,768,128]{3,2,1,0:T(8,128)S(1)} %pad_maximum_fusion.base_ref), custom_call_target="tpu_custom_call" | custom-call | tf_op jit(solution)/shard_map/tables/pallas_call | solution.py:131
  24.2 0.0 copy-start
  24.2 1.4 %copy-done = bf16[2,768,768]{2,1,0:T(8,128)(2,1)} copy-done((bf16[2,768,768]{2,1,0:T(8,128)(2,1)}, bf16[2,768,768]{2,1,0:T(8,128)(2,1)S(1)}, u32[]{:S(2)}) %copy-start) | copy-done | bytes 2359320
  25.6 0.0 copy-start.1
  25.6 1.4 %copy-done.1 = bf16[2,768,768]{2,1,0:T(8,128)(2,1)} copy-done((bf16[2,768,768]{2,1,0:T(8,128)(2,1)}, bf16[2,768,768]{2,1,0:T(8,128)(2,1)S(1)}, u32[]{:S(2)}) %copy-start.1) | copy-done | bytes 2359320
  27.1 0.1 fusion.20
  27.2 0.2 sine_multiply_fusion
  27.5 0.1 bitcast_add_fusion
  27.5 0.2 fusion.17.refs_6_
  27.7 0.5 broadcast_select_fusion.refs_4_
  28.2 28.3 %all-to-all-done = f32[64,48,128]{2,1,0:T(8,128)S(1)} async-done(((f32[64,48,128]{2,1,0:T(8,128)}), f32[64,48,128]{2,1,0:T(8,128)S(1)}, u32[]{:S(2)}, u32[]{:S(2)}) %all-to-all-start) | async-done | bytes 1572896 | tf_op jit(solution)/shard_map/all_to_all | solution.py:319
  56.5 5.1 %criterion.1 = (f32[184,128]{1,0:T(8,128)S(1)}, f32[184,128]{1,0:T(8,128)S(1)}, f32[184,128]{1,0:T(8,128)S(1)}, f32[184,128]{1,0:T(8,128)S(1)}) custom-call(s32[1]{0:T(128)} %bitcast.refs_0_.me_ref, f32[3072,128]{1,0:T(8,128)S(1)} %bitcast.14, bf16[2,768,768]{2,1,0:T(8,128)(2,1)} %copy-done, bf16[2,768,768]{2,1,0:T(8,128)(2,1)} %copy-done.1, ...), custom_call_target="tpu_custom_call" | custom-call | tf_op jit(solution)/shard_map/criterion/pallas_call | solution.py:286
  61.6 4.0 %collective-permute-start = (f32[184,128]{1,0:T(8,128)S(1)}, f32[184,128]{1,0:T(8,128)S(1)}, u32[]{:S(2)}, u32[]{:S(2)}) collective-permute-start(f32[184,128]{1,0:T(8,128)S(1)} %get-tuple-element.14), channel_id=1, source_target_pairs={{0,1},{1,0},{2,3},{3,2},{4,5},{5,4},{6,7},{7,6},{8,9},{9,8},{10,11... | collective-permute-start | bytes 282632 | tf_op jit(solution)/shard_map/ppermute | solution.py:327
  65.6 0.6 collective-permute-start.1
  66.2 1.9 %collective-permute-start.2 = (f32[184,128]{1,0:T(8,128)S(1)}, f32[184,128]{1,0:T(8,128)S(1)}, u32[]{:S(2)}, u32[]{:S(2)}) collective-permute-start(f32[184,128]{1,0:T(8,128)S(1)} %get-tuple-element.16), channel_id=1, source_target_pairs={{0,3},{1,2},{2,1},{3,0},{4,7},{5,6},{6,5},{7,4},{8,11},{9,10},{10,... | collective-permute-start | bytes 282632 | tf_op jit(solution)/shard_map/ppermute | solution.py:327
  68.1 0.6 collective-permute-done.refs_1_
  68.7 7.1 %collective-permute-done.1.refs_2_ = f32[184,128]{1,0:T(8,128)S(1)} collective-permute-done((f32[184,128]{1,0:T(8,128)S(1)}, f32[184,128]{1,0:T(8,128)S(1)}, u32[]{:S(2)}, u32[]{:S(2)}) %collective-permute-start.1) | collective-permute-done | bytes 94240 | tf_op jit(solution)/shard_map/ppermute | solution.py:327
  75.8 0.0 collective-permute-done.2.refs_3_
  75.8 1.1 %assemble.1 = f32[2,30,4,384]{3,2,1,0:T(4,128)} custom-call(s32[1]{0:T(128)} %bitcast.refs_0_.me_ref, f32[184,128]{1,0:T(8,128)S(1)} %get-tuple-element.13.refs_0_, f32[184,128]{1,0:T(8,128)S(1)} %collective-permute-done.refs_1_, f32[184,128]{1,0:T(8,128)S(1)} %collective-permute-done.1.refs_2_, f32[184,128]{1,0:T(8,128)S(1)} %collective-permute-done.2.refs_3_), custom_call_target="tpu_custom_call" | custom-call | tf_op jit(solution)/shard_map/assemble/pallas_call | solution.py:305
  (16 shorter events, 0.2 us)
Async XLA Ops:
  2.7 53.8 %all-to-all-start = ((f32[64,48,128]{2,1,0:T(8,128)}), f32[64,48,128]{2,1,0:T(8,128)S(1)}, u32[]{:S(2)}, u32[]{:S(2)}) async-start(f32[64,48,128]{2,1,0:T(8,128)} %pack.1), calls=%async_computation | async-start | bytes 3145728 | tf_op jit(solution)/shard_map/all_to_all | solution.py:319
  24.2 1.4 %copy-start = (bf16[2,768,768]{2,1,0:T(8,128)(2,1)}, bf16[2,768,768]{2,1,0:T(8,128)(2,1)S(1)}, u32[]{:S(2)}) copy-start(bf16[2,768,768]{2,1,0:T(8,128)(2,1)S(1)} %get-tuple-element.11.refs_2_) | copy-start | bytes 7077892
  25.6 1.4 %copy-start.1 = (bf16[2,768,768]{2,1,0:T(8,128)(2,1)}, bf16[2,768,768]{2,1,0:T(8,128)(2,1)S(1)}, u32[]{:S(2)}) copy-start(bf16[2,768,768]{2,1,0:T(8,128)(2,1)S(1)} %get-tuple-element.12.refs_3_) | copy-start | bytes 7077892
  61.6 7.1 %collective-permute-start = (f32[184,128]{1,0:T(8,128)S(1)}, f32[184,128]{1,0:T(8,128)S(1)}, u32[]{:S(2)}, u32[]{:S(2)}) collective-permute-start(f32[184,128]{1,0:T(8,128)S(1)} %get-tuple-element.14), channel_id=1, source_target_pairs={{0,1},{1,0},{2,3},{3,2},{4,5},{5,4},{6,7},{7,6},{8,9},{9,8},{10,11... | collective-permute-start | bytes 282632 | tf_op jit(solution)/shard_map/ppermute | solution.py:327
  65.6 10.2 %collective-permute-start.1 = (f32[184,128]{1,0:T(8,128)S(1)}, f32[184,128]{1,0:T(8,128)S(1)}, u32[]{:S(2)}, u32[]{:S(2)}) collective-permute-start(f32[184,128]{1,0:T(8,128)S(1)} %get-tuple-element.15), channel_id=1, source_target_pairs={{0,2},{1,3},{2,0},{3,1},{4,6},{5,7},{6,4},{7,5},{8,10},{9,11},{10,... | collective-permute-start | bytes 282632 | tf_op jit(solution)/shard_map/ppermute | solution.py:327
  66.2 9.6 %collective-permute-start.2 = (f32[184,128]{1,0:T(8,128)S(1)}, f32[184,128]{1,0:T(8,128)S(1)}, u32[]{:S(2)}, u32[]{:S(2)}) collective-permute-start(f32[184,128]{1,0:T(8,128)S(1)} %get-tuple-element.16), channel_id=1, source_target_pairs={{0,3},{1,2},{2,1},{3,0},{4,7},{5,6},{6,5},{7,4},{8,11},{9,10},{10,... | collective-permute-start | bytes 282632 | tf_op jit(solution)/shard_map/ppermute | solution.py:327
